TPU v7x, 32 devices: a whole 2x2x4 slice. The times are simulated.
32 devices in a mesh: row: 4 (over x, core), col: 4 (over z), pt: 2 (over y).
Axes of the slice: x: 2, y: 2, z: 4, core: 2. Of those that a mesh axis runs over, the one named last changes fastest.
Arguments:
- first_factors: int32 [32, 1024, 1024], P('pt', 'row', 'col'), may hold values from 0 to 12288
- second_factors: int32 [32, 1024, 1024], P('pt', 'row', 'col'), may hold values from 0 to 12288
Outputs:
- scaled_product: float32 [45, 1024, 1024], P(None, ('row', 'pt'), 'col')
All inputs are finite; a program needn't handle non-finite values.
Results may differ from a plain program's by a relative error of at most 0.0003.
Values may be sent and summed in bfloat16 or wider, within the bound.
A program may use at most 128 MiB of HBM per device.

v0:
```python
import jax
import jax.numpy as jnp
import numpy as np
from jax import lax
from jax.sharding import PartitionSpec as P

DEG = 16
modulus = 12289
digit_base = 128


def primitive_root():
    for candidate in range(2, modulus):
        if pow(candidate, 6144, modulus) != 1 and pow(candidate, 4096, modulus) != 1:
            return candidate
    return 0


def make_table(order_size, row_count, column_count, inverse):
    generator = primitive_root()
    root_value = pow(generator, (modulus - 1) // order_size, modulus)
    scaling = 1
    if inverse:
        root_value = pow(root_value, modulus - 2, modulus)
        scaling = pow(order_size, modulus - 2, modulus)
    entries = [
        [
            pow(root_value, row_index * column_index % order_size, modulus) * scaling % modulus
            for column_index in range(column_count)
        ]
        for row_index in range(row_count)
    ]
    return np.array(entries, dtype=np.int64)


def value_digits(values):
    high_digit = values // digit_base
    return (
        high_digit.astype(jnp.bfloat16),
        (values - digit_base * high_digit).astype(jnp.bfloat16),
    )


def combine(high_high, high_low, low_high, low_low):
    top_part = high_high.astype(jnp.int32) % modulus
    middle_part = (high_low.astype(jnp.int32) + low_high.astype(jnp.int32)) % modulus
    return (
        top_part * (digit_base * digit_base) % modulus
        + middle_part * digit_base
        + low_low.astype(jnp.int32)
    ) % modulus


def transform(matrix_table, coefs):
    slot_count = coefs.shape[0]
    flat_coefs = coefs.reshape(slot_count, -1)
    table_high = jnp.asarray(matrix_table // digit_base, dtype=jnp.bfloat16)
    table_low = jnp.asarray(matrix_table % digit_base, dtype=jnp.bfloat16)
    data_high, data_low = value_digits(flat_coefs)

    def product_of(left_part, right_part):
        return jnp.dot(left_part, right_part, preferred_element_type=jnp.float32)

    mixed_values = combine(
        product_of(table_high, data_high),
        product_of(table_high, data_low),
        product_of(table_low, data_high),
        product_of(table_low, data_low),
    )
    return mixed_values.reshape(matrix_table.shape[0], coefs.shape[1], coefs.shape[2])


def batched_product(left_part, right_part):
    return jnp.einsum("bik,bkj->bij", left_part, right_part, preferred_element_type=jnp.float32)


def digit_sum(totals, left_digits, right_digits):
    return (
        totals[0] + batched_product(left_digits[0], right_digits[0]),
        totals[1] + batched_product(left_digits[0], right_digits[1]),
        totals[2] + batched_product(left_digits[1], right_digits[0]),
        totals[3] + batched_product(left_digits[1], right_digits[1]),
    )


def pointwise(left_values, right_values):
    left_points, right_points = (
        lax.all_to_all(
            lax.all_to_all(
                left_values.astype(jnp.float32), "col", split_axis=0, concat_axis=2, tiled=True
            ),
            "pt",
            split_axis=0,
            concat_axis=1,
            tiled=True,
        ),
        lax.all_to_all(
            lax.all_to_all(
                right_values.astype(jnp.float32), "col", split_axis=0, concat_axis=2, tiled=True
            ),
            "pt",
            split_axis=0,
            concat_axis=1,
            tiled=True,
        ),
    )
    left_digits = value_digits(left_points.astype(jnp.int32))
    right_digits = value_digits(right_points.astype(jnp.int32))
    zeros_init = jnp.zeros(left_points.shape, jnp.float32)
    column_parts = tuple((digit_part for digit_part in left_digits))
    totals = digit_sum(
        (zeros_init, zeros_init, zeros_init, zeros_init),
        column_parts,
        (
            lax.all_gather(right_digits[0], "row", axis=1, tiled=True),
            lax.all_gather(right_digits[1], "row", axis=1, tiled=True),
        ),
    )
    product_values = combine(totals[0], totals[1], totals[2], totals[3]).astype(jnp.float32)
    arrived = lax.all_to_all(
        lax.all_to_all(product_values, "col", split_axis=2, concat_axis=0, tiled=True),
        "pt",
        split_axis=1,
        concat_axis=0,
        tiled=True,
    )
    col_count = lax.axis_size("col")
    pt_count = lax.axis_size("pt")
    local_count = arrived.shape[0] // (col_count * pt_count)
    returned = arrived.reshape(pt_count, col_count, local_count, arrived.shape[1], arrived.shape[2])
    returned = returned.transpose(1, 0, 2, 3, 4).reshape(arrived.shape)
    return returned.astype(jnp.int32)


def local(first_factors, second_factors):
    forward_one = make_table(2 * DEG, 2 * DEG, DEG, False)
    inverse_one = make_table(2 * DEG, 2 * DEG, 2 * DEG, True)
    forward_two = make_table(4 * DEG, 4 * DEG, 2 * DEG, False)
    inverse_two = make_table(4 * DEG, 3 * DEG - 3, 4 * DEG, True)
    first_entries, second_entries = (
        lax.all_to_all(
            first_factors.astype(jnp.float32), "pt", split_axis=1, concat_axis=0, tiled=True
        ),
        lax.all_to_all(
            second_factors.astype(jnp.float32), "pt", split_axis=1, concat_axis=0, tiled=True
        ),
    )
    first_entries = first_entries.astype(jnp.int32)
    second_entries = second_entries.astype(jnp.int32)
    left_values = jnp.concatenate(
        [transform(forward_one, first_entries[:DEG]), transform(forward_one, first_entries[DEG:])],
        0,
    )
    right_values = jnp.concatenate(
        [
            transform(forward_one, second_entries[:DEG]),
            transform(forward_one, second_entries[DEG:]),
        ],
        0,
    )
    products = pointwise(left_values, right_values)
    first_product = transform(inverse_one, products[: 2 * DEG])
    second_product = transform(inverse_one, products[2 * DEG :])
    upper_values = transform(forward_two, first_product)
    lower_values = transform(forward_two[:, :DEG], second_product[DEG:])
    result_coefficients = transform(inverse_two, pointwise(upper_values, lower_values))
    return result_coefficients.astype(jnp.float32) / 12289.0


def reduce_centred(values):
    return values - 12289.0 * jnp.round(values * (1.0 / 12289.0))


def centred_digits(values):
    high_digit = jnp.round(values * (1.0 / 128.0))
    return (high_digit.astype(jnp.bfloat16), (values - 128.0 * high_digit).astype(jnp.bfloat16))


def combine_centred(high_high, middle, low_low):
    upper_part = reduce_centred(reduce_centred(high_high) * 128.0 + middle)
    return reduce_centred(upper_part * 128.0 + low_low)


def table_digits(matrix_table):
    centred = np.where(matrix_table > modulus // 2, matrix_table - modulus, matrix_table)
    high_digit = np.round(centred / 128.0)
    return (high_digit, centred - 128.0 * high_digit)


def centred_transform(table_high, table_low, coefs):
    data_high, data_low = centred_digits(coefs.astype(jnp.float32))
    table_high = jnp.asarray(table_high, dtype=jnp.bfloat16)
    table_low = jnp.asarray(table_low, dtype=jnp.bfloat16)

    def product_of(left_part, right_part):
        return jnp.einsum("ts,sab->tab", left_part, right_part, preferred_element_type=jnp.float32)

    middle = product_of(
        jnp.concatenate([table_high, table_low], 1), jnp.concatenate([data_low, data_high], 0)
    )
    return combine_centred(
        product_of(table_high, data_high), middle, product_of(table_low, data_low)
    )


def column_pointwise(left_values, right_values):
    right_points = lax.all_to_all(
        right_values.astype(jnp.int16), "col", split_axis=0, concat_axis=2, tiled=True
    )
    right_points = lax.all_gather(right_points, "row", axis=1, tiled=True)
    left_points = lax.all_to_all(
        left_values.astype(jnp.int16), "col", split_axis=0, concat_axis=2, tiled=True
    )
    left_high, left_low = centred_digits(left_points.astype(jnp.float32))
    right_high, right_low = centred_digits(right_points.astype(jnp.float32))
    middle = batched_product(left_high, right_low) + batched_product(left_low, right_high)
    product_values = combine_centred(
        batched_product(left_high, right_high), middle, batched_product(left_low, right_low)
    )
    return lax.all_to_all(
        product_values.astype(jnp.int16), "col", split_axis=2, concat_axis=0, tiled=True
    )


def pair_local(first_factors, second_factors):
    forward_one = table_digits(make_table(2 * DEG, 2 * DEG, DEG, False))
    inverse_one = table_digits(make_table(2 * DEG, 2 * DEG, 2 * DEG, True))
    forward_two = table_digits(make_table(4 * DEG, 4 * DEG, 2 * DEG, False))
    inverse_two = table_digits(make_table(4 * DEG, 3 * DEG - 3, 4 * DEG, True))
    half_points = 2 * DEG
    place = lax.axis_index("pt")
    products = column_pointwise(
        centred_transform(*forward_one, centre(first_factors)),
        centred_transform(*forward_one, centre(second_factors)),
    )
    own_product = centred_transform(*inverse_one, products).astype(jnp.int16)
    both_products = lax.all_gather(own_product, "pt", axis=0, tiled=True)
    first_product = both_products[: 2 * DEG]
    shifted = both_products[3 * DEG :]
    own_tables = [
        lax.dynamic_slice_in_dim(
            jnp.asarray(digit, dtype=jnp.bfloat16), place * half_points, half_points, 0
        )
        for digit in forward_two
    ]
    upper_values = centred_transform(*own_tables, first_product)
    lower_values = centred_transform(*[digit[:, :DEG] for digit in own_tables], shifted)
    products_two = column_pointwise(upper_values, lower_values)
    all_points = lax.all_to_all(products_two, "pt", split_axis=1, concat_axis=0, tiled=True)
    result = centred_transform(*inverse_two, all_points)
    return jnp.where(result < 0.0, result + 12289.0, result) / 12289.0


def centre(values):
    return jnp.where(values > modulus // 2, values - modulus, values)


def solution(mesh):
    in_specs = (P("pt", "row", "col"), P("pt", "row", "col"))
    out_specs = P(None, ("row", "pt"), "col")
    body = pair_local if mesh.shape["pt"] == 2 else local
    return jax.shard_map(body, mesh=mesh, in_specs=in_specs, out_specs=out_specs, check_vma=False)
```

profile of v0, /device:TPU:0, one launch (start us, length us, event | category | flops | bytes accessed | tf_op | source)
XLA Modules:
  0.0 1258.8 jit_solution(4259190581243966023)
XLA Ops:
  0.0 5.5 fusion.68
  8.2 7.1 subtract_convert_fusion.8
  19.6 6.6 all-to-all-start
  26.2 5.4 fusion.67
  34.3 7.1 subtract_convert_fusion.7
  45.8 73.8 %all-to-all-done = s16[32,256,256]{2,1,0:T(8,128)(2,1)} async-done(((s16[32,256,256]{2,1,0:T(8,128)(2,1)}), s16[32,256,256]{2,1,0:T(8,128)(2,1)}, u32[]{:S(2)}, u32[]{:S(2)}) %all-to-all-start) | async-done | bytes 4194336 | tf_op jit(solution)/shard_map/all_to_all | solution.py:211
  119.6 5.3 all-to-all-start.1
  124.9 6.8 convert.12
  131.8 12.0 copy.111
  143.8 10.8 reshape.16
  154.6 63.0 %all-to-all-done.1 = s16[32,256,256]{2,1,0:T(8,128)(2,1)} async-done(((s16[32,256,256]{2,1,0:T(8,128)(2,1)}), s16[32,256,256]{2,1,0:T(8,128)(2,1)}, u32[]{:S(2)}, u32[]{:S(2)}) %all-to-all-start.1) | async-done | bytes 4194336 | tf_op jit(solution)/shard_map/all_to_all | solution.py:207
  217.6 7.4 copy.113
  225.0 7.9 all_to_all.71
  232.9 105.4 %all-gather.3 = s16[8,1024,1024]{2,1,0:T(8,128)(2,1)} all-gather(s16[8,256,1024]{2,1,0:T(8,128)(2,1)} %all_to_all.71), channel_id=1, replica_groups=mesh['row'=4,'col'=4,'pt'=2] {'row'}, dimensions={1}, use_global_device_ids=true | all-gather | bytes 20971520 | tf_op jit(solution)/shard_map/all_gather | solution.py:210
  338.4 16.5 %fusion.14 = f32[8,256,1024]{2,1,0:T(8,128)} fusion(s16[8,1024,1024]{2,1,0:T(8,128)(2,1)} %all-gather.3, f32[8,256,1024]{2,1,0:T(8,128)} %reshape.16), kind=kOutput, calls=%fused_computation.16 | convolution fusion | flops 4334813184 | bytes 33554432 | tf_op jit(solution)/shard_map/bik,bkj->bij/dot_general | solution.py:74
  354.9 17.6 %fusion.12 = f32[8,256,1024]{2,1,0:T(8,128)} fusion(s16[8,1024,1024]{2,1,0:T(8,128)(2,1)} %all-gather.3, f32[8,256,1024]{2,1,0:T(8,128)} %reshape.16), kind=kOutput, calls=%fused_computation.15 | convolution fusion | flops 4339007488 | bytes 33554432 | tf_op jit(solution)/shard_map/bik,bkj->bij/dot_general | solution.py:74
  372.5 18.3 %fusion.20 = f32[8,256,1024]{2,1,0:T(8,128)} fusion(s16[8,1024,1024]{2,1,0:T(8,128)(2,1)} %all-gather.3, f32[8,256,1024]{2,1,0:T(8,128)} %reshape.16), kind=kOutput, calls=%fused_computation.23 | convolution fusion | flops 4355784704 | bytes 33554432 | tf_op jit(solution)/shard_map/bik,bkj->bij/dot_general | solution.py:74
  390.8 25.6 %subtract_convert_fusion.5 = s16[8,256,1024]{2,1,0:T(8,128)(2,1)} fusion(f32[8,256,1024]{2,1,0:T(8,128)} %fusion.20, f32[8,256,1024]{2,1,0:T(8,128)} %fusion.12, f32[8,256,1024]{2,1,0:T(8,128)} %fusion.14, s16[8,1024,1024]{2,1,0:T(8,128)(2,1)} %all-gather.3, f32[8,256,1024]{2,1,0:T(8,128)} %reshape.16), kind=kOutput, calls=%fused_computation.59 | convolution fusion | flops 4389339136 | bytes 54525952 | tf_op jit(solution)/shard_map/bik,bkj->bij/dot_general | solution.py:74
  416.3 7.3 copy.76
  423.6 5.1 all-to-all-start.2
  428.8 94.0 %all-to-all-done.2 = s16[8,256,1024]{1,0,2:T(8,128)(2,1)} async-done(((s16[8,256,1024]{1,0,2:T(8,128)(2,1)}), s16[8,256,1024]{1,0,2:T(8,128)(2,1)}, u32[]{:S(2)}, u32[]{:S(2)}) %all-to-all-start.2) | async-done | bytes 4194336 | tf_op jit(solution)/shard_map/all_to_all | solution.py:220
  522.8 6.5 convert.13
  529.3 10.5 copy.77
  547.0 8.1 subtract_convert_fusion.4
  555.1 92.8 %all-gather.4 = s16[64,256,256]{2,0,1:T(8,128)(2,1)S(1)} all-gather(s16[32,256,256]{2,0,1:T(8,128)(2,1)} %subtract_convert_fusion.4), channel_id=1, replica_groups=mesh['row'=4,'col'=4,'pt'=2] {'pt'}, dimensions={0}, use_global_device_ids=true | all-gather | bytes 12582912 | tf_op jit(solution)/shard_map/all_gather | solution.py:237
  657.1 10.0 subtract_convert_fusion.3
  671.3 5.1 all-to-all-start.3
  682.9 8.5 subtract_convert_fusion.2
  691.5 6.5 copy.82
  698.0 70.7 %all-to-all-done.3 = s16[32,256,256]{2,1,0:T(8,128)(2,1)} async-done(((s16[32,256,256]{2,1,0:T(8,128)(2,1)}), s16[32,256,256]{2,1,0:T(8,128)(2,1)}, u32[]{:S(2)}, u32[]{:S(2)}) %all-to-all-start.3) | async-done | bytes 4194336 | tf_op jit(solution)/shard_map/all_to_all | solution.py:211
  768.7 5.1 all-to-all-start.4
  773.8 6.8 convert.14
  780.6 12.0 copy.110
  792.6 10.8 reshape.18
  803.4 63.1 %all-to-all-done.4 = s16[32,256,256]{2,1,0:T(8,128)(2,1)} async-done(((s16[32,256,256]{2,1,0:T(8,128)(2,1)}), s16[32,256,256]{2,1,0:T(8,128)(2,1)}, u32[]{:S(2)}, u32[]{:S(2)}) %all-to-all-start.4) | async-done | bytes 4194336 | tf_op jit(solution)/shard_map/all_to_all | solution.py:207
  866.5 7.4 copy.112
  874.0 7.9 all_to_all.77
  881.9 104.5 %all-gather.5 = s16[8,1024,1024]{2,1,0:T(8,128)(2,1)} all-gather(s16[8,256,1024]{2,1,0:T(8,128)(2,1)} %all_to_all.77), channel_id=1, replica_groups=mesh['row'=4,'col'=4,'pt'=2] {'row'}, dimensions={1}, use_global_device_ids=true | all-gather | bytes 20971520 | tf_op jit(solution)/shard_map/all_gather | solution.py:210
  986.4 16.5 %fusion.10 = f32[8,256,1024]{2,1,0:T(8,128)} fusion(s16[8,1024,1024]{2,1,0:T(8,128)(2,1)} %all-gather.5, f32[8,256,1024]{2,1,0:T(8,128)} %reshape.18), kind=kOutput, calls=%fused_computation.14 | convolution fusion | flops 4334813184 | bytes 33554432 | tf_op jit(solution)/shard_map/bik,bkj->bij/dot_general | solution.py:74
  1002.9 17.6 %fusion.8 = f32[8,256,1024]{2,1,0:T(8,128)} fusion(s16[8,1024,1024]{2,1,0:T(8,128)(2,1)} %all-gather.5, f32[8,256,1024]{2,1,0:T(8,128)} %reshape.18), kind=kOutput, calls=%fused_computation.13 | convolution fusion | flops 4339007488 | bytes 33554432 | tf_op jit(solution)/shard_map/bik,bkj->bij/dot_general | solution.py:74
  1020.5 18.3 %fusion.16 = f32[8,256,1024]{2,1,0:T(8,128)} fusion(s16[8,1024,1024]{2,1,0:T(8,128)(2,1)} %all-gather.5, f32[8,256,1024]{2,1,0:T(8,128)} %reshape.18), kind=kOutput, calls=%fused_computation.21 | convolution fusion | flops 4355784704 | bytes 33554432 | tf_op jit(solution)/shard_map/bik,bkj->bij/dot_general | solution.py:74
  1038.7 25.6 %subtract_convert_fusion = s16[8,256,1024]{2,1,0:T(8,128)(2,1)} fusion(f32[8,256,1024]{2,1,0:T(8,128)} %fusion.16, f32[8,256,1024]{2,1,0:T(8,128)} %fusion.8, f32[8,256,1024]{2,1,0:T(8,128)} %fusion.10, s16[8,1024,1024]{2,1,0:T(8,128)(2,1)} %all-gather.5, f32[8,256,1024]{2,1,0:T(8,128)} %reshape.18), kind=kOutput, calls=%fused_computation.52 | convolution fusion | flops 4389339136 | bytes 54525952 | tf_op jit(solution)/shard_map/bik,bkj->bij/dot_general | solution.py:74
  1064.3 7.3 copy.84
  1071.5 99.7 %all_to_all.90 = s16[8,256,1024]{1,0,2:T(8,128)(2,1)} all-to-all(s16[8,256,1024]{1,0,2:T(8,128)(2,1)} %copy.84), channel_id=1, replica_groups=mesh['row'=4,'col'=4,'pt'=2] {'col'}, dimensions={2} | all-to-all | bytes 8388608 | tf_op jit(solution)/shard_map/all_to_all | solution.py:220
  1171.2 7.9 copy.86
  1183.6 50.0 %all_to_all.91 = s16[32,256,256]{2,0,1:T(8,128)(2,1)S(1)} all-to-all(s16[32,256,256]{2,0,1:T(8,128)(2,1)S(1)} %copy.87), channel_id=1, replica_groups=mesh['row'=4,'col'=4,'pt'=2] {'pt'}, dimensions={1} | all-to-all | bytes 8388608 | tf_op jit(solution)/shard_map/all_to_all | solution.py:249
  1246.9 5.5 fusion.48
  1252.4 6.0 copy.90
  (54 shorter events, 58.9 us)
Async XLA Ops:
  0.0 5.5 copy-start.3
  0.0 6.8 copy-start.2
  6.7 1.4 copy-start.11
  19.6 100.0 %all-to-all-start = ((s16[32,256,256]{2,1,0:T(8,128)(2,1)}), s16[32,256,256]{2,1,0:T(8,128)(2,1)}, u32[]{:S(2)}, u32[]{:S(2)}) async-start(s16[32,256,256]{2,1,0:T(8,128)(2,1)} %copy.69), calls=%async_computation | async-start | bytes 8388608 | tf_op jit(solution)/shard_map/all_to_all | solution.py:211
  119.6 98.0 %all-to-all-start.1 = ((s16[32,256,256]{2,1,0:T(8,128)(2,1)}), s16[32,256,256]{2,1,0:T(8,128)(2,1)}, u32[]{:S(2)}, u32[]{:S(2)}) async-start(s16[32,256,256]{2,1,0:T(8,128)(2,1)} %copy.74), calls=%async_computation.1 | async-start | bytes 8388608 | tf_op jit(solution)/shard_map/all_to_all | solution.py:207
  416.3 12.5 copy-start.1
  416.3 12.5 copy-start.4
  423.6 99.2 %all-to-all-start.2 = ((s16[8,256,1024]{1,0,2:T(8,128)(2,1)}), s16[8,256,1024]{1,0,2:T(8,128)(2,1)}, u32[]{:S(2)}, u32[]{:S(2)}) async-start(s16[8,256,1024]{1,0,2:T(8,128)(2,1)} %copy.76), calls=%async_computation.2 | async-start | bytes 8388608 | tf_op jit(solution)/shard_map/all_to_all | solution.py:220
  539.8 4.5 copy-start.8
  544.3 1.3 copy-start.7
  545.5 1.5 copy-start.10
  648.0 9.1 copy-start
  671.3 97.4 %all-to-all-start.3 = ((s16[32,256,256]{2,1,0:T(8,128)(2,1)}), s16[32,256,256]{2,1,0:T(8,128)(2,1)}, u32[]{:S(2)}, u32[]{:S(2)}) async-start(s16[32,256,256]{2,1,0:T(8,128)(2,1)} %copy.78), calls=%async_computation.3 | async-start | bytes 8388608 | tf_op jit(solution)/shard_map/all_to_all | solution.py:211
  676.4 4.3 slice-start
  679.4 2.2 slice-start.1
  768.7 97.8 %all-to-all-start.4 = ((s16[32,256,256]{2,1,0:T(8,128)(2,1)}), s16[32,256,256]{2,1,0:T(8,128)(2,1)}, u32[]{:S(2)}, u32[]{:S(2)}) async-start(s16[32,256,256]{2,1,0:T(8,128)(2,1)} %copy.82), calls=%async_computation.4 | async-start | bytes 8388608 | tf_op jit(solution)/shard_map/all_to_all | solution.py:207
  1242.3 2.2 copy-start.5
  1244.4 1.0 copy-start.6
  1245.4 1.5 copy-start.9
where the time goes:
time: 1270 us; the launch traced here: 1260 us
  blocking collectives  452 us (36%)
  waiting for transfers between devices  364 us (29%)
  matrix products  221 us (17%)
  local copies, waits for them, and re-layouts  148 us (12%)
  other arithmetic  45.2 us (4%)
  starting transfers between devices  27.2 us (2%)
    all_gather x2, blocking collectives, column_pointwise(): right_points = lax.all_gather(right_points, 'row', axis=1, tiled=True)  210 us
    dot_general x8, matrix products, batched_product(): jnp.einsum('bik,bkj->bij', left_part, right_part, preferred_element_type=...  156 us
    all_to_all x2, waiting for transfers between devices, column_pointwise(): lax.all_to_all(left_values.astype(jnp.int16), 'col', split_axis=0, concat...  144 us
    all_to_all x2, waiting for transfers between devices, column_pointwise(): lax.all_to_all(right_values.astype(jnp.int16), 'col', split_axis=0, conca...  126 us
    all_to_all x1, blocking collectives, column_pointwise(): lax.all_to_all(product_values.astype(jnp.int16), 'col', split_axis=2, con...  99.7 us
    all_to_all x1, waiting for transfers between devices, column_pointwise(): lax.all_to_all(product_values.astype(jnp.int16), 'col', split_axis=2, con...  94 us
    all_gather x1, blocking collectives, pair_local(): both_products = lax.all_gather(own_product, 'pt', axis=0, tiled=True)  92.8 us
    dot_general x18, matrix products, product_of(): jnp.einsum('ts,sab->tab', left_part, right_part, preferred_element_type=j...  65.3 us
  transfers between devices with their start and end apart: 5, of which 5 were waited for; matrix products, arithmetic and copies ran while one was open for 8% of the time, Pallas kernels for 0%

commit v1 on v0

--- a/solution.py
+++ b/solution.py
@@ -204,9 +204,21 @@
 
 
 def column_pointwise(left_values, right_values):
-    right_points = lax.all_to_all(
-        right_values.astype(jnp.int16), "col", split_axis=0, concat_axis=2, tiled=True
-    )
+    x = right_values.astype(jnp.int16)
+    ways, here = (lax.axis_size("col"), lax.axis_index("col"))
+    width = x.shape[0] // ways
+    shape = list(x.shape)
+    shape[0] = width
+    height = shape[2]
+    shape[2] = height * ways
+    right_points = jnp.zeros(shape, x.dtype)
+    for mask in range(ways):
+        part = lax.dynamic_slice_in_dim(x, (here ^ mask) * width, width, axis=0)
+        if mask:
+            part = lax.ppermute(part, "col", [(d, d ^ mask) for d in range(ways)])
+        right_points = lax.dynamic_update_slice_in_dim(
+            right_points, part, (here ^ mask) * height, axis=2
+        )
     right_points = lax.all_gather(right_points, "row", axis=1, tiled=True)
     left_points = lax.all_to_all(
         left_values.astype(jnp.int16), "col", split_axis=0, concat_axis=2, tiled=True

time: 1270 us -> 1170 us (0.921)
  waiting for transfers between devices: 364 us -> 228 us
  starting transfers between devices: 27.2 us -> 66.6 us
  local copies, waits for them, and re-layouts: 148 us -> 123 us
  blocking collectives: 452 us -> 476 us
    all_to_all x2, waiting for transfers between devices: 144 us -> 0.01 us  [column_pointwise(): lax.all_to_all(left_values.astype(jnp.int16), 'col', split_axis=0, concat...]
    ppermute x0 -> x6, waiting for transfers between devices: none -> 133 us  [column_pointwise(): part = lax.ppermute(part, 'col', [(d, d ^ mask) for d in range(ways)])]
    all_to_all x2 -> x0, waiting for transfers between devices: 126 us -> none  [column_pointwise(): lax.all_to_all(right_values.astype(jnp.int16), 'col', split_axis=0, conca...]
    all_to_all x1, starting transfers between devices: 5.15 us -> 46.4 us  [column_pointwise(): lax.all_to_all(product_values.astype(jnp.int16), 'col', split_axis=2, con...]
    all_to_all x1, blocking collectives: 99.7 us -> 140 us  [column_pointwise(): lax.all_to_all(product_values.astype(jnp.int16), 'col', split_axis=2, con...]
    all_to_all x4 -> x0, local copies, waits for them, and re-layouts: 30.7 us -> none  [column_pointwise(): lax.all_to_all(right_values.astype(jnp.int16), 'col', split_axis=0, conca...]
    all_gather x2, blocking collectives: 210 us -> 191 us  [column_pointwise(): right_points = lax.all_gather(right_points, 'row', axis=1, tiled=True)]
  transfers between devices with their start and end apart: 5 -> 9, of which waited for: 5 -> 5; matrix products, arithmetic and copies ran while one was open for 8% -> 4% of each run, Pallas kernels for 0% -> 0%
where the time goes in v1:
time: 1170 us
  blocking collectives  476 us (41%)
  matrix products  232 us (20%)
  waiting for transfers between devices  228 us (19%)
  local copies, waits for them, and re-layouts  123 us (11%)
  starting transfers between devices  66.6 us (6%)
  other arithmetic  42.6 us (4%)
    all_gather x2, blocking collectives, column_pointwise(): right_points = lax.all_gather(right_points, 'row', axis=1, tiled=True)  191 us
    dot_general x8, matrix products, batched_product(): jnp.einsum('bik,bkj->bij', left_part, right_part, preferred_element_type=...  161 us
    all_to_all x1, blocking collectives, column_pointwise(): lax.all_to_all(product_values.astype(jnp.int16), 'col', split_axis=2, con...  140 us
    ppermute x6, waiting for transfers between devices, column_pointwise(): part = lax.ppermute(part, 'col', [(d, d ^ mask) for d in range(ways)])  133 us
    all_to_all x1, waiting for transfers between devices, column_pointwise(): lax.all_to_all(product_values.astype(jnp.int16), 'col', split_axis=2, con...  94.6 us
    all_gather x1, blocking collectives, pair_local(): both_products = lax.all_gather(own_product, 'pt', axis=0, tiled=True)  93.4 us
    dot_general x18, matrix products, product_of(): jnp.einsum('ts,sab->tab', left_part, right_part, preferred_element_type=j...  70.9 us
    all_to_all x1, blocking collectives, pair_local(): lax.all_to_all(products_two, 'pt', split_axis=1, concat_axis=0, tiled=True)  50.8 us
  transfers between devices with their start and end apart: 9, of which 5 were waited for; matrix products, arithmetic and copies ran while one was open for 4% of the time, Pallas kernels for 0%

profile of v1, /device:TPU:0, one launch (start us, length us, event | category | flops | bytes accessed | tf_op | source)
XLA Modules:
  0.0 1168.8 jit_solution(11263585071370423219)
XLA Ops:
  0.0 6.8 fusion.67
  10.0 7.1 subtract_convert_fusion.7
  30.4 7.3 subtract_convert_fusion.8
  37.6 4.4 copy.85
  42.0 5.1 all-to-all-start
  48.0 19.8 %collective-permute-done = s16[8,256,256]{2,0,1:T(8,128)(2,1)} collective-permute-done((s16[8,256,256]{2,0,1:T(8,128)(2,1)}, s16[8,256,256]{2,0,1:T(8,128)(2,1)}, u32[]{:S(2)}, u32[]{:S(2)}) %collective-permute-start) | collective-permute-done | bytes 1048608 | tf_op jit(solution)/shard_map/ppermute | solution.py:218
  69.4 46.8 %collective-permute-done.1 = s16[8,256,256]{2,0,1:T(8,128)(2,1)} collective-permute-done((s16[8,256,256]{2,0,1:T(8,128)(2,1)S(1)}, s16[8,256,256]{2,0,1:T(8,128)(2,1)}, u32[]{:S(2)}, u32[]{:S(2)}) %collective-permute-start.1) | collective-permute-done | bytes 1048608 | tf_op jit(solution)/shard_map/ppermute | solution.py:218
  119.3 96.1 %all-gather.3 = s16[8,1024,1024]{2,1,0:T(8,128)(2,1)} all-gather(s16[8,256,1024]{2,1,0:T(8,128)(2,1)S(1)} %copy_dynamic-update-slice_fusion.4), channel_id=1, replica_groups=mesh['row'=4,'col'=4,'pt'=2] {'row'}, dimensions={1}, use_global_device_ids=true | all-gather | bytes 20971520 | tf_op jit(solution)/shard_map/all_gather | solution.py:222
  215.4 6.8 convert.12
  222.2 12.0 %copy.137 = f32[4,8,256,256]{3,0,2,1:T(4,128)} copy(f32[4,8,256,256]{3,2,1,0:T(8,128)} %convert.12) | data formatting | bytes 16777216 | tf_op jit(solution)/shard_map/convert_element_type | solution.py:226
  234.2 11.2 reshape.16
  245.5 16.5 %fusion.14 = f32[8,256,1024]{2,1,0:T(8,128)} fusion(s16[8,1024,1024]{2,1,0:T(8,128)(2,1)} %all-gather.3, f32[8,256,1024]{2,1,0:T(8,128)} %reshape.16), kind=kOutput, calls=%fused_computation.16 | convolution fusion | flops 4334813184 | bytes 33554432 | tf_op jit(solution)/shard_map/bik,bkj->bij/dot_general | solution.py:74
  262.0 17.6 %fusion.12 = f32[8,256,1024]{2,1,0:T(8,128)} fusion(s16[8,1024,1024]{2,1,0:T(8,128)(2,1)} %all-gather.3, f32[8,256,1024]{2,1,0:T(8,128)} %reshape.16), kind=kOutput, calls=%fused_computation.15 | convolution fusion | flops 4339007488 | bytes 33554432 | tf_op jit(solution)/shard_map/bik,bkj->bij/dot_general | solution.py:74
  279.6 18.9 %fusion.22 = f32[8,256,1024]{2,1,0:T(8,128)} fusion(s16[8,1024,1024]{2,1,0:T(8,128)(2,1)} %all-gather.3, f32[8,256,1024]{2,1,0:T(8,128)} %reshape.16), kind=kOutput, calls=%fused_computation.24 | convolution fusion | flops 4351590400 | bytes 33554432 | tf_op jit(solution)/shard_map/bik,bkj->bij/dot_general | solution.py:74
  298.5 27.5 %subtract_convert_fusion.5 = s16[8,256,1024]{2,1,0:T(8,128)(2,1)} fusion(f32[8,256,1024]{2,1,0:T(8,128)} %fusion.22, f32[8,256,1024]{2,1,0:T(8,128)} %fusion.12, f32[8,256,1024]{2,1,0:T(8,128)} %fusion.14, s16[8,1024,1024]{2,1,0:T(8,128)(2,1)} %all-gather.3, f32[8,256,1024]{2,1,0:T(8,128)} %reshape.16), kind=kOutput, calls=%fused_computation.59 | convolution fusion | flops 4393533440 | bytes 54525952 | tf_op jit(solution)/shard_map/bik,bkj->bij/dot_general | solution.py:74
  325.9 7.3 copy.94
  333.2 46.4 %all-to-all-start.1 = ((s16[8,256,1024]{1,0,2:T(8,128)(2,1)}), s16[8,256,1024]{1,0,2:T(8,128)(2,1)}, u32[]{:S(2)}, u32[]{:S(2)}) async-start(s16[8,256,1024]{1,0,2:T(8,128)(2,1)} %copy.94), calls=%async_computation.1 | async-start | bytes 8388608 | tf_op jit(solution)/shard_map/all_to_all | solution.py:232
  379.7 94.6 %all-to-all-done.1 = s16[8,256,1024]{1,0,2:T(8,128)(2,1)} async-done(((s16[8,256,1024]{1,0,2:T(8,128)(2,1)}), s16[8,256,1024]{1,0,2:T(8,128)(2,1)}, u32[]{:S(2)}, u32[]{:S(2)}) %all-to-all-start.1) | async-done | bytes 4194336 | tf_op jit(solution)/shard_map/all_to_all | solution.py:232
  474.3 6.5 convert.13
  480.8 10.5 copy.95
  491.3 4.5 fusion.46
  498.6 8.1 subtract_convert_fusion.4
  506.7 93.4 %all-gather.4 = s16[64,256,256]{2,0,1:T(8,128)(2,1)S(1)} all-gather(s16[32,256,256]{2,0,1:T(8,128)(2,1)} %subtract_convert_fusion.4), channel_id=1, replica_groups=mesh['row'=4,'col'=4,'pt'=2] {'pt'}, dimensions={0}, use_global_device_ids=true | all-gather | bytes 12582912 | tf_op jit(solution)/shard_map/all_gather | solution.py:249
  603.1 4.6 fusion.84
  609.0 4.6 fusion.81
  614.9 10.4 subtract_convert_fusion.2
  625.2 4.3 constant_dynamic-slice_fusion.2
  635.2 10.1 subtract_convert_fusion.3
  645.4 4.4 copy.96
  649.8 5.0 all-to-all-start.2
  655.7 22.0 %collective-permute-done.3 = s16[8,256,256]{2,0,1:T(8,128)(2,1)} collective-permute-done((s16[8,256,256]{2,0,1:T(8,128)(2,1)}, s16[8,256,256]{2,0,1:T(8,128)(2,1)}, u32[]{:S(2)}, u32[]{:S(2)}) %collective-permute-start.3) | collective-permute-done | bytes 1048608 | tf_op jit(solution)/shard_map/ppermute | solution.py:218
  679.3 44.9 %collective-permute-done.4 = s16[8,256,256]{2,0,1:T(8,128)(2,1)} collective-permute-done((s16[8,256,256]{2,0,1:T(8,128)(2,1)}, s16[8,256,256]{2,0,1:T(8,128)(2,1)}, u32[]{:S(2)}, u32[]{:S(2)}) %collective-permute-start.4) | collective-permute-done | bytes 1048608 | tf_op jit(solution)/shard_map/ppermute | solution.py:218
  727.4 95.2 %all-gather.5 = s16[8,1024,1024]{2,1,0:T(8,128)(2,1)} all-gather(s16[8,256,1024]{2,1,0:T(8,128)(2,1)S(1)} %copy_dynamic-update-slice_fusion), channel_id=1, replica_groups=mesh['row'=4,'col'=4,'pt'=2] {'row'}, dimensions={1}, use_global_device_ids=true | all-gather | bytes 20971520 | tf_op jit(solution)/shard_map/all_gather | solution.py:222
  822.5 6.8 convert.14
  829.4 12.0 %copy.136 = f32[4,8,256,256]{3,0,2,1:T(4,128)} copy(f32[4,8,256,256]{3,2,1,0:T(8,128)} %convert.14) | data formatting | bytes 16777216 | tf_op jit(solution)/shard_map/convert_element_type | solution.py:226
  841.4 11.2 reshape.18
  852.6 16.5 %fusion.10 = f32[8,256,1024]{2,1,0:T(8,128)} fusion(s16[8,1024,1024]{2,1,0:T(8,128)(2,1)} %all-gather.5, f32[8,256,1024]{2,1,0:T(8,128)} %reshape.18), kind=kOutput, calls=%fused_computation.14 | convolution fusion | flops 4334813184 | bytes 33554432 | tf_op jit(solution)/shard_map/bik,bkj->bij/dot_general | solution.py:74
  869.1 17.6 %fusion.8 = f32[8,256,1024]{2,1,0:T(8,128)} fusion(s16[8,1024,1024]{2,1,0:T(8,128)(2,1)} %all-gather.5, f32[8,256,1024]{2,1,0:T(8,128)} %reshape.18), kind=kOutput, calls=%fused_computation.13 | convolution fusion | flops 4339007488 | bytes 33554432 | tf_op jit(solution)/shard_map/bik,bkj->bij/dot_general | solution.py:74
  886.7 18.9 %fusion.18 = f32[8,256,1024]{2,1,0:T(8,128)} fusion(s16[8,1024,1024]{2,1,0:T(8,128)(2,1)} %all-gather.5, f32[8,256,1024]{2,1,0:T(8,128)} %reshape.18), kind=kOutput, calls=%fused_computation.22 | convolution fusion | flops 4351590400 | bytes 33554432 | tf_op jit(solution)/shard_map/bik,bkj->bij/dot_general | solution.py:74
  905.6 27.5 %subtract_convert_fusion = s16[8,256,1024]{2,1,0:T(8,128)(2,1)} fusion(f32[8,256,1024]{2,1,0:T(8,128)} %fusion.18, f32[8,256,1024]{2,1,0:T(8,128)} %fusion.8, f32[8,256,1024]{2,1,0:T(8,128)} %fusion.10, s16[8,1024,1024]{2,1,0:T(8,128)(2,1)} %all-gather.5, f32[8,256,1024]{2,1,0:T(8,128)} %reshape.18), kind=kOutput, calls=%fused_computation.52 | convolution fusion | flops 4393533440 | bytes 54525952 | tf_op jit(solution)/shard_map/bik,bkj->bij/dot_general | solution.py:74
  933.0 7.3 copy.104
  940.3 140.3 %all_to_all.54 = s16[8,256,1024]{1,0,2:T(8,128)(2,1)} all-to-all(s16[8,256,1024]{1,0,2:T(8,128)(2,1)} %copy.104), channel_id=1, replica_groups=mesh['row'=4,'col'=4,'pt'=2] {'col'}, dimensions={2} | all-to-all | bytes 8388608 | tf_op jit(solution)/shard_map/all_to_all | solution.py:232
  1080.6 7.9 copy.106
  1088.5 4.5 copy.107
  1093.0 50.8 %all_to_all.55 = s16[32,256,256]{2,0,1:T(8,128)(2,1)S(1)} all-to-all(s16[32,256,256]{2,0,1:T(8,128)(2,1)S(1)} %copy.107), channel_id=1, replica_groups=mesh['row'=4,'col'=4,'pt'=2] {'pt'}, dimensions={1} | all-to-all | bytes 8388608 | tf_op jit(solution)/shard_map/all_to_all | solution.py:261
  1147.6 4.9 copy.109
  1157.1 5.5 fusion.48
  1162.6 6.0 copy.110
  (67 shorter events, 50.0 us)
Async XLA Ops:
  0.0 6.8 copy-start.5
  0.0 8.1 copy-start.4
  6.8 1.6 copy-start
  8.1 1.9 copy-start.13
  17.0 7.2 copy-start.2
  18.6 49.2 %collective-permute-start = (s16[8,256,256]{2,0,1:T(8,128)(2,1)}, s16[8,256,256]{2,0,1:T(8,128)(2,1)}, u32[]{:S(2)}, u32[]{:S(2)}) collective-permute-start(s16[8,256,256]{2,0,1:T(8,128)(2,1)} %get-tuple-element.21), channel_id=1, source_target_pairs={{0,2},{2,0},{4,6},{6,4},{1,3},{3,1},{5,7},{7,5},{8,10},{10,8},{12,... | collective-permute-start | bytes 3145736 | tf_op jit(solution)/shard_map/ppermute | solution.py:218
  21.7 94.5 %collective-permute-start.1 = (s16[8,256,256]{2,0,1:T(8,128)(2,1)S(1)}, s16[8,256,256]{2,0,1:T(8,128)(2,1)}, u32[]{:S(2)}, u32[]{:S(2)}) collective-permute-start(s16[8,256,256]{2,0,1:T(8,128)(2,1)S(1)} %get-tuple-element.20), channel_id=1, source_target_pairs={{0,4},{2,6},{4,0},{6,2},{1,5},{3,7},{5,1},{7,3},{8,12},{10,14},{12... | collective-permute-start | bytes 3145736 | tf_op jit(solution)/shard_map/ppermute | solution.py:218
  24.2 93.5 %collective-permute-start.2 = (s16[8,256,256]{2,0,1:T(8,128)(2,1)S(1)}, s16[8,256,256]{2,0,1:T(8,128)(2,1)}, u32[]{:S(2)}, u32[]{:S(2)}) collective-permute-start(s16[8,256,256]{2,0,1:T(8,128)(2,1)S(1)} %get-tuple-element.19), channel_id=1, source_target_pairs={{0,6},{2,4},{4,2},{6,0},{1,7},{3,5},{5,3},{7,1},{8,14},{10,12},{12... | collective-permute-start | bytes 3145736 | tf_op jit(solution)/shard_map/ppermute | solution.py:218
  42.0 173.4 %all-to-all-start = ((s16[32,256,256]{2,1,0:T(8,128)(2,1)}), s16[32,256,256]{2,1,0:T(8,128)(2,1)}, u32[]{:S(2)}, u32[]{:S(2)}) async-start(s16[32,256,256]{2,1,0:T(8,128)(2,1)} %copy.85), calls=%async_computation | async-start | bytes 8388608 | tf_op jit(solution)/shard_map/all_to_all | solution.py:223
  325.9 53.7 %copy-start.3 = (bf16[64,32]{1,0:T(8,128)(2,1)S(1)}, bf16[64,32]{1,0:T(8,128)(2,1)}, u32[]{:S(2)}) copy-start(bf16[64,32]{1,0:T(8,128)(2,1)} %constant.24.clone) | copy-start | bytes 12292
  325.9 53.8 %copy-start.6 = (bf16[64,32]{1,0:T(8,128)(2,1)S(1)}, bf16[64,32]{1,0:T(8,128)(2,1)}, u32[]{:S(2)}) copy-start(bf16[64,32]{1,0:T(8,128)(2,1)} %constant.23.clone) | copy-start | bytes 12292
  333.2 141.1 %all-to-all-start.1 = ((s16[8,256,1024]{1,0,2:T(8,128)(2,1)}), s16[8,256,1024]{1,0,2:T(8,128)(2,1)}, u32[]{:S(2)}, u32[]{:S(2)}) async-start(s16[8,256,1024]{1,0,2:T(8,128)(2,1)} %copy.94), calls=%async_computation.1 | async-start | bytes 8388608 | tf_op jit(solution)/shard_map/all_to_all | solution.py:232
  491.3 4.5 copy-start.10
  495.8 1.3 copy-start.9
  497.1 1.5 copy-start.12
  629.5 48.2 %collective-permute-start.3 = (s16[8,256,256]{2,0,1:T(8,128)(2,1)}, s16[8,256,256]{2,0,1:T(8,128)(2,1)}, u32[]{:S(2)}, u32[]{:S(2)}) collective-permute-start(s16[8,256,256]{2,0,1:T(8,128)(2,1)} %get-tuple-element.15), channel_id=1, source_target_pairs={{0,2},{2,0},{4,6},{6,4},{1,3},{3,1},{5,7},{7,5},{8,10},{10,8},{12,... | collective-permute-start | bytes 3145736 | tf_op jit(solution)/shard_map/ppermute | solution.py:218
  629.5 94.7 %collective-permute-start.4 = (s16[8,256,256]{2,0,1:T(8,128)(2,1)}, s16[8,256,256]{2,0,1:T(8,128)(2,1)}, u32[]{:S(2)}, u32[]{:S(2)}) collective-permute-start(s16[8,256,256]{2,0,1:T(8,128)(2,1)} %get-tuple-element.14), channel_id=1, source_target_pairs={{0,4},{2,6},{4,0},{6,2},{1,5},{3,7},{5,1},{7,3},{8,12},{10,14},{12... | collective-permute-start | bytes 3145736 | tf_op jit(solution)/shard_map/ppermute | solution.py:218
  631.5 94.3 %collective-permute-start.5 = (s16[8,256,256]{2,0,1:T(8,128)(2,1)}, s16[8,256,256]{2,0,1:T(8,128)(2,1)}, u32[]{:S(2)}, u32[]{:S(2)}) collective-permute-start(s16[8,256,256]{2,0,1:T(8,128)(2,1)} %get-tuple-element.13), channel_id=1, source_target_pairs={{0,6},{2,4},{4,2},{6,0},{1,7},{3,5},{5,3},{7,1},{8,14},{10,12},{12... | collective-permute-start | bytes 3145736 | tf_op jit(solution)/shard_map/ppermute | solution.py:218
  649.8 5.6 copy-start.1
  649.8 172.8 %all-to-all-start.2 = ((s16[32,256,256]{2,1,0:T(8,128)(2,1)}), s16[32,256,256]{2,1,0:T(8,128)(2,1)}, u32[]{:S(2)}, u32[]{:S(2)}) async-start(s16[32,256,256]{2,1,0:T(8,128)(2,1)} %copy.96), calls=%async_computation.2 | async-start | bytes 8388608 | tf_op jit(solution)/shard_map/all_to_all | solution.py:223
  1152.4 2.2 copy-start.7
  1154.6 1.0 copy-start.8
  1155.6 1.5 copy-start.11
